TPU v7x, 32 devices: a whole 2x2x4 slice. The times are simulated.
32 devices in a mesh: tm: 8 (over z, x), pack: 4 (over y, core).
Axes of the slice: x: 2, y: 2, z: 4, core: 2. Of those that a mesh axis runs over, the one named last changes fastest.
Arguments:
- queries: bfloat16 [4, 4096, 1024], P('pack', 'tm'), may hold values from -8 to 8
- keys: bfloat16 [4, 4096, 1024], P('pack', 'tm'), may hold values from -8 to 8
- values: bfloat16 [4, 4096, 1024], P('pack', 'tm'), may hold values from -6 to 6
- w_out: bfloat16 [1024, 1024], replicated, may hold values from -0.1875 to 0.1875
- norm_gain: float32 [1024], replicated, may hold values from 0.1 to 1.9
- block_owner: int32 [4, 32, 1], P('pack', 'tm'), may hold values from 0 to 3; in each aligned block of 4 rows (0 to 3, 4 to 7, ..., all dimensions but the last counted through in order) at most 2 rows name the same one
- block_base: int32 [4, 32], P('pack', 'tm'), may hold values from 0 to 112
- frame_offset: int32 [4, 32, 128], P('pack', 'tm'), may hold values from 0 to 15, never falling along the last dimension, each value on 1 to 16 neighbouring positions
Outputs:
- encoded: bfloat16 [4, 4096, 1024], P('pack', 'tm')
- pooled: bfloat16 [4, 1024, 1024], P('pack', 'tm')
Inputs may be any that keep to these rules, and one draw needn't show every extreme that they name: `block_owner`: among the 4 blocks of one device (aligned runs of the list), at most 2 name the same owner. `frame_offset`: within each block of 128 frames the offsets never fall and each of 0 to 15 occurs.
All inputs are finite; a program needn't handle non-finite values.
Results may differ from a plain program's by a relative error of at most 0.008.
Values may be sent and summed in bfloat16 or wider, within the bound.
No kernel may reach another device: no remote copies, remote signals or barrier semaphores. Data moves between devices by JAX's collectives and lax.ppermute only.
A program may use at most 128 MiB of HBM per device.

v0:
```python
import math
import jax
import jax.numpy as jnp
from jax import lax
from jax.sharding import PartitionSpec as P

HEADS = 16
LANDMARKS = 256
BLOCK = 128
POOL_DEV = 128


def mix_heads(query_rows, mark_keys, mark_values, head_count):
    row_count, model_width = query_rows.shape
    head_dim = model_width // head_count
    query_heads = query_rows.reshape(row_count, head_count, head_dim)
    key_heads = mark_keys.reshape(-1, head_count, head_dim)
    value_heads = mark_values.reshape(-1, head_count, head_dim)
    scores = jnp.einsum(
        "nhe,mhe->nhm", query_heads, key_heads, preferred_element_type=jnp.float32
    ) * head_dim ** (-0.5)
    weights = jnp.exp(scores - jnp.max(scores, axis=-1, keepdims=True))
    totals = jnp.sum(weights, axis=-1)
    blended = jnp.einsum(
        "nhm,mhe->nhe",
        weights.astype(jnp.bfloat16),
        value_heads,
        preferred_element_type=jnp.float32,
    )
    return (blended / totals[..., None]).reshape(row_count, model_width).astype(jnp.bfloat16)


def mix_blocked(query_rows, mark_keys, mark_values, head_count):
    row_count, model_width = query_rows.shape
    row_block = math.gcd(row_count, 1024)
    stacked = query_rows.reshape(row_count // row_block, row_block, model_width)
    mixed_rows = lax.map(
        lambda frame_block: mix_heads(frame_block, mark_keys, mark_values, head_count), stacked
    )
    return mixed_rows.reshape(row_count, model_width)


def local(queries, keys, values, w_out, norm_gain, block_owner, block_base, frame_offset):
    frame_q = queries[0]
    frame_k = keys[0]
    frame_v = values[0]
    frame_count, model_width = frame_q.shape
    span = frame_count // LANDMARKS
    mark_queries = jnp.mean(
        frame_q.reshape(LANDMARKS, span, model_width), axis=1, dtype=jnp.float32
    ).astype(jnp.bfloat16)
    mark_keys = jnp.mean(
        frame_k.reshape(LANDMARKS, span, model_width), axis=1, dtype=jnp.float32
    ).astype(jnp.bfloat16)
    mark_values = mix_heads(mark_queries, frame_k, frame_v, HEADS)
    spread_q, spread_k, spread_v = (
        lax.all_to_all(frame_q, "tm", split_axis=1, concat_axis=0, tiled=True),
        lax.all_to_all(mark_keys, "tm", split_axis=1, concat_axis=0, tiled=True),
        lax.all_to_all(mark_values, "tm", split_axis=1, concat_axis=0, tiled=True),
    )
    local_heads = HEADS // lax.axis_size("tm")
    head_result = mix_blocked(spread_q, spread_k, spread_v, local_heads)
    attended = lax.all_to_all(head_result, "tm", split_axis=0, concat_axis=1, tiled=True)
    projected = jnp.dot(attended, w_out, preferred_element_type=jnp.float32)
    scaled = projected * lax.rsqrt(jnp.mean(projected * projected, axis=-1, keepdims=True) + 1e-06)
    encoded = (scaled * norm_gain).astype(jnp.bfloat16)
    pack_count = lax.axis_size("pack")
    owners = block_owner[0, :, 0]
    block_count = owners.shape[0]
    slot_count = max(2, 2 * block_count // pack_count)
    pack_range = jnp.arange(pack_count, dtype=jnp.int32)
    dest_hits = (owners[:, None] == pack_range[None, :]).astype(jnp.int32)
    slot_rank = jnp.sum((jnp.cumsum(dest_hits, axis=0) - dest_hits) * dest_hits, axis=1)
    chosen = (owners[None, None, :] == pack_range[:, None, None]) & (
        slot_rank[None, None, :] == jnp.arange(slot_count, dtype=jnp.int32)[None, :, None]
    )
    filled = jnp.any(chosen, axis=-1)
    source_block = jnp.sum(
        chosen.astype(jnp.int32) * jnp.arange(block_count, dtype=jnp.int32)[None, None, :], axis=-1
    )
    frame_blocks = encoded.reshape(block_count, BLOCK, model_width)
    offsets = frame_offset[0]
    block_bases = block_base[0]
    sent_rows = jnp.where(
        filled[..., None, None],
        jnp.take(frame_blocks, source_block, axis=0),
        jnp.zeros((), jnp.bfloat16),
    )
    row_targets = jnp.take(block_bases, source_block)[..., None] + jnp.take(
        offsets, source_block, axis=0
    )
    sent_targets = jnp.where(filled[..., None], row_targets, -1).astype(jnp.bfloat16)
    got_rows, got_targets = (
        lax.all_to_all(sent_rows, "pack", split_axis=0, concat_axis=0, tiled=True),
        lax.all_to_all(sent_targets, "pack", split_axis=0, concat_axis=0, tiled=True),
    )
    pool_rows = jnp.arange(POOL_DEV, dtype=jnp.int32).astype(jnp.bfloat16)
    placing = got_targets[:, :, None, :] == pool_rows[None, None, :, None]
    pool_sums = jnp.einsum(
        "scrf,scfd->rd", placing.astype(jnp.bfloat16), got_rows, preferred_element_type=jnp.float32
    )
    pool_counts = jnp.sum(placing.astype(jnp.float32), axis=(0, 1, 3))
    pooled = (pool_sums / jnp.maximum(pool_counts, 1.0)[:, None]).astype(jnp.bfloat16)
    return (encoded[None], pooled[None])


def solution(mesh):
    return jax.shard_map(
        local,
        mesh=mesh,
        in_specs=(
            P("pack", "tm", None),
            P("pack", "tm", None),
            P("pack", "tm", None),
            P(),
            P(),
            P("pack", "tm", None),
            P("pack", "tm"),
            P("pack", "tm", None),
        ),
        out_specs=(P("pack", "tm", None), P("pack", "tm", None)),
        check_vma=False,
    )
```

profile of v0, /device:TPU:0, one launch (start us, length us, event | category | flops | bytes accessed | tf_op | source)
XLA Modules:
  0.0 267.6 jit_solution(12814046430353551243)
XLA Ops:
  0.7 3.6 %reshape.165 = f32[256,2,1024]{2,1,0:T(2,128)} reshape(bf16[1,512,1024]{2,1,0:T(8,128)(2,1)} %param.11) | data formatting | bytes 3145728 | tf_op jit(solution)/shard_map/convert_element_type | solution.py:52
  4.2 5.1 %reduce_sum.74 = f32[256,1024]{1,0:T(8,128)} reduce(f32[256,2,1024]{2,1,0:T(2,128)} %reshape.165, f32[]{:T(128)} %constant.55.clone.1), dimensions={1}, to_apply=%region_0.0 | reduce | flops 262144 | bytes 3145732 | tf_op jit(solution)/shard_map/reduce_sum | solution.py:52
  9.3 2.1 multiply_convert_fusion.2
  11.4 2.1 copy.80
  13.5 7.3 %all-to-all-start.1 = ((bf16[256,8,128]{0,2,1:T(8,128)(2,1)}), bf16[256,8,128]{0,2,1:T(8,128)(2,1)}, u32[]{:S(2)}, u32[]{:S(2)}) async-start(bf16[256,8,128]{0,2,1:T(8,128)(2,1)} %bitcast.126), calls=%async_computation.1 | async-start | bytes 1048576 | tf_op jit(solution)/shard_map/all_to_all | solution.py:58
  20.8 1.3 copy.83
  22.1 3.5 %reshape.166 = f32[256,2,1024]{2,1,0:T(2,128)} reshape(bf16[1,512,1024]{2,1,0:T(8,128)(2,1)} %param.10) | data formatting | bytes 3145728 | tf_op jit(solution)/shard_map/convert_element_type | solution.py:49
  25.6 5.1 %reduce_sum.75 = f32[256,1024]{1,0:T(8,128)} reduce(f32[256,2,1024]{2,1,0:T(2,128)} %reshape.166, f32[]{:T(128)} %constant.55.clone.1), dimensions={1}, to_apply=%region_1.0 | reduce | flops 262144 | bytes 3145732 | tf_op jit(solution)/shard_map/reduce_sum | solution.py:49
  30.7 2.1 multiply_convert_fusion.1
  32.8 2.0 copy.82
  34.8 2.4 bitcast_reduce_fusion.1
  37.2 3.2 %copy-done.3 = f32[16,256,512]{2,1,0:T(8,128)} copy-done((f32[16,256,512]{2,1,0:T(8,128)}, f32[16,256,512]{2,1,0:T(8,128)S(1)}, u32[]{:S(2)}) %copy-start.3) | copy-done | bytes 8388632
  40.5 2.0 fusion.16
  42.5 2.4 copy.84
  44.8 6.1 %divide_convert_fusion = bf16[256,16,64]{0,2,1:T(8,128)(2,1)} fusion(bf16[512,16,64]{0,2,1:T(8,128)(2,1)} %bitcast.129, f32[16,256,512]{2,1,0:T(8,128)} %copy-done.3, f32[256,16]{0,1:T(8,128)S(1)} %get-tuple-element.71, f32[256,16]{0,1:T(8,128)S(1)} %fusion.16), kind=kOutput, calls=%fused_computation.30 | convolution fusion | flops 275251200 | bytes 9994240 | tf_op jit(solution)/shard_map/nhm,mhe->nhe/dot_general | solution.py:24
  51.0 6.0 %all-to-all-start.2 = ((bf16[256,8,128]{0,2,1:T(8,128)(2,1)}), bf16[256,8,128]{0,2,1:T(8,128)(2,1)}, u32[]{:S(2)}, u32[]{:S(2)}) async-start(bf16[256,8,128]{0,2,1:T(8,128)(2,1)} %bitcast.131), calls=%async_computation.2 | async-start | bytes 1048576 | tf_op jit(solution)/shard_map/all_to_all | solution.py:59
  57.0 1.3 copy.78
  58.3 12.7 %all-to-all-done.2 = bf16[256,8,128]{0,2,1:T(8,128)(2,1)} async-done(((bf16[256,8,128]{0,2,1:T(8,128)(2,1)}), bf16[256,8,128]{0,2,1:T(8,128)(2,1)}, u32[]{:S(2)}, u32[]{:S(2)}) %all-to-all-start.2) | async-done | bytes 524320 | tf_op jit(solution)/shard_map/all_to_all | solution.py:59
  71.0 4.2 %all-to-all-start = ((bf16[512,8,128]{0,2,1:T(8,128)(2,1)}), bf16[512,8,128]{0,2,1:T(8,128)(2,1)}, u32[]{:S(2)}, u32[]{:S(2)}) async-start(bf16[512,8,128]{0,2,1:T(8,128)(2,1)} %bitcast.124), calls=%async_computation | async-start | bytes 2097152 | tf_op jit(solution)/shard_map/all_to_all | solution.py:57
  75.3 1.3 copy.81
  76.9 1.9 copy.103
  78.8 21.8 %all-to-all-done = bf16[512,8,128]{0,2,1:T(8,128)(2,1)} async-done(((bf16[512,8,128]{0,2,1:T(8,128)(2,1)}), bf16[512,8,128]{0,2,1:T(8,128)(2,1)}, u32[]{:S(2)}, u32[]{:S(2)}) %all-to-all-start) | async-done | bytes 1048608 | tf_op jit(solution)/shard_map/all_to_all | solution.py:57
  100.5 2.3 copy.79
  102.8 89.4 %while.10 = (s32[]{:T(128)}, bf16[4,1024,128]{2,1,0:T(8,128)(2,1)}, bf16[4,1024,128]{2,1,0:T(8,128)(2,1)}, bf16[2048,128]{0,1:T(8,128)(2,1)S(1)}, bf16[2048,128]{0,1:T(8,128)(2,1)}, /*index=5*/s32[]{:T(128)}) while((s32[]{:T(128)}, bf16[4,1024,128]{2,1,0:T(8,128)(2,1)}, bf16[4,1024,128]{2,1,0:T(8,128)(2,1)}, bf16[2048,128]{0,1:T(8,128)(2,1)S(1)}, ...), condition=%wide.region_7.8_spmd, body=%wide.region_4.7_spmd.sunk | while | flops 1107554304 | bytes 121151608 | solution.py:37
  102.8 1.0 constant_dynamic-slice_fusion.2
  104.0 2.5 bitcast_reduce_fusion.3
  106.5 5.7 %copy-done.2 = f32[2,1024,2048]{2,1,0:T(8,128)} copy-done((f32[2,1024,2048]{2,1,0:T(8,128)}, f32[2,1024,2048]{2,1,0:T(8,128)S(1)}, u32[]{:S(2)}) %copy-start.2) | copy-done | bytes 16777240 | tf_op jit(solution)/shard_map/while
  112.2 3.3 %fusion.67 = f32[1024,2]{0,1:T(2,128)S(1)} fusion(f32[2,1024,2048]{2,1,0:T(8,128)S(1)} %get-tuple-element.108, f32[1024,2]{0,1:T(2,128)S(1)} %get-tuple-element.109), kind=kLoop, calls=%fused_computation.6.clone.1 | loop fusion | flops 12580864 | bytes 16793600 | tf_op jit(solution)/shard_map/while/body/eval_jaxpr/reduce_sum | solution.py:23
  115.4 8.9 %fusion.68 = bf16[1024,2,64]{0,2,1:T(8,128)(2,1)S(1)} fusion(bf16[2048,2,64]{0,2,1:T(8,128)(2,1)} %bitcast.110, f32[2,1024,2048]{2,1,0:T(8,128)} %copy-done.2, f32[1024,2]{0,1:T(2,128)S(1)} %get-tuple-element.109, f32[1024,2]{0,1:T(2,128)S(1)} %fusion.67), kind=kOutput, calls=%fused_computation.11.clone.1 | convolution fusion | flops 549715968 | bytes 17580032 | tf_op jit(solution)/shard_map/while/body/eval_jaxpr/nhm,mhe->nhe/dot_general | solution.py:24
  124.5 0.7 constant_dynamic-update-slice_fusion.2
  125.2 1.0 constant_dynamic-slice_fusion.2
  126.3 2.5 bitcast_reduce_fusion.3
  128.8 5.7 %copy-done.2 = f32[2,1024,2048]{2,1,0:T(8,128)} copy-done((f32[2,1024,2048]{2,1,0:T(8,128)}, f32[2,1024,2048]{2,1,0:T(8,128)S(1)}, u32[]{:S(2)}) %copy-start.2) | copy-done | bytes 16777240 | tf_op jit(solution)/shard_map/while
  134.5 3.3 %fusion.67 = f32[1024,2]{0,1:T(2,128)S(1)} fusion(f32[2,1024,2048]{2,1,0:T(8,128)S(1)} %get-tuple-element.108, f32[1024,2]{0,1:T(2,128)S(1)} %get-tuple-element.109), kind=kLoop, calls=%fused_computation.6.clone.1 | loop fusion | flops 12580864 | bytes 16793600 | tf_op jit(solution)/shard_map/while/body/eval_jaxpr/reduce_sum | solution.py:23
  137.8 8.8 %fusion.68 = bf16[1024,2,64]{0,2,1:T(8,128)(2,1)S(1)} fusion(bf16[2048,2,64]{0,2,1:T(8,128)(2,1)} %bitcast.110, f32[2,1024,2048]{2,1,0:T(8,128)} %copy-done.2, f32[1024,2]{0,1:T(2,128)S(1)} %get-tuple-element.109, f32[1024,2]{0,1:T(2,128)S(1)} %fusion.67), kind=kOutput, calls=%fused_computation.11.clone.1 | convolution fusion | flops 549715968 | bytes 17580032 | tf_op jit(solution)/shard_map/while/body/eval_jaxpr/nhm,mhe->nhe/dot_general | solution.py:24
  146.8 0.7 constant_dynamic-update-slice_fusion.2
  147.5 1.0 constant_dynamic-slice_fusion.2
  148.7 2.5 bitcast_reduce_fusion.3
  151.1 5.7 %copy-done.2 = f32[2,1024,2048]{2,1,0:T(8,128)} copy-done((f32[2,1024,2048]{2,1,0:T(8,128)}, f32[2,1024,2048]{2,1,0:T(8,128)S(1)}, u32[]{:S(2)}) %copy-start.2) | copy-done | bytes 16777240 | tf_op jit(solution)/shard_map/while
  156.9 3.3 %fusion.67 = f32[1024,2]{0,1:T(2,128)S(1)} fusion(f32[2,1024,2048]{2,1,0:T(8,128)S(1)} %get-tuple-element.108, f32[1024,2]{0,1:T(2,128)S(1)} %get-tuple-element.109), kind=kLoop, calls=%fused_computation.6.clone.1 | loop fusion | flops 12580864 | bytes 16793600 | tf_op jit(solution)/shard_map/while/body/eval_jaxpr/reduce_sum | solution.py:23
  160.1 8.8 %fusion.68 = bf16[1024,2,64]{0,2,1:T(8,128)(2,1)S(1)} fusion(bf16[2048,2,64]{0,2,1:T(8,128)(2,1)} %bitcast.110, f32[2,1024,2048]{2,1,0:T(8,128)} %copy-done.2, f32[1024,2]{0,1:T(2,128)S(1)} %get-tuple-element.109, f32[1024,2]{0,1:T(2,128)S(1)} %fusion.67), kind=kOutput, calls=%fused_computation.11.clone.1 | convolution fusion | flops 549715968 | bytes 17580032 | tf_op jit(solution)/shard_map/while/body/eval_jaxpr/nhm,mhe->nhe/dot_general | solution.py:24
  169.1 0.7 constant_dynamic-update-slice_fusion.2
  169.9 1.0 constant_dynamic-slice_fusion.2
  171.0 2.5 bitcast_reduce_fusion.3
  173.5 5.7 %copy-done.2 = f32[2,1024,2048]{2,1,0:T(8,128)} copy-done((f32[2,1024,2048]{2,1,0:T(8,128)}, f32[2,1024,2048]{2,1,0:T(8,128)S(1)}, u32[]{:S(2)}) %copy-start.2) | copy-done | bytes 16777240 | tf_op jit(solution)/shard_map/while
  179.2 3.3 %fusion.67 = f32[1024,2]{0,1:T(2,128)S(1)} fusion(f32[2,1024,2048]{2,1,0:T(8,128)S(1)} %get-tuple-element.108, f32[1024,2]{0,1:T(2,128)S(1)} %get-tuple-element.109), kind=kLoop, calls=%fused_computation.6.clone.1 | loop fusion | flops 12580864 | bytes 16793600 | tf_op jit(solution)/shard_map/while/body/eval_jaxpr/reduce_sum | solution.py:23
  182.4 8.8 %fusion.68 = bf16[1024,2,64]{0,2,1:T(8,128)(2,1)S(1)} fusion(bf16[2048,2,64]{0,2,1:T(8,128)(2,1)} %bitcast.110, f32[2,1024,2048]{2,1,0:T(8,128)} %copy-done.2, f32[1024,2]{0,1:T(2,128)S(1)} %get-tuple-element.109, f32[1024,2]{0,1:T(2,128)S(1)} %fusion.67), kind=kOutput, calls=%fused_computation.11.clone.1 | convolution fusion | flops 549715968 | bytes 17580032 | tf_op jit(solution)/shard_map/while/body/eval_jaxpr/nhm,mhe->nhe/dot_general | solution.py:24
  191.5 0.7 constant_dynamic-update-slice_fusion.2
  192.2 3.7 %all-to-all-start.3 = ((bf16[8,512,128]{2,1,0:T(8,128)(2,1)}), bf16[8,512,128]{2,1,0:T(8,128)(2,1)S(1)}, u32[]{:S(2)}, u32[]{:S(2)}) async-start(bf16[8,512,128]{2,1,0:T(8,128)(2,1)} %bitcast.128), calls=%async_computation.3 | async-start | bytes 2097152 | tf_op jit(solution)/shard_map/all_to_all | solution.py:63
  196.6 0.6 gather_fusion
  197.8 0.6 gather_fusion.1
  198.5 0.7 select_convert_fusion
  199.1 22.5 %all-to-all-done.3 = bf16[8,512,128]{2,1,0:T(8,128)(2,1)S(1)} async-done(((bf16[8,512,128]{2,1,0:T(8,128)(2,1)}), bf16[8,512,128]{2,1,0:T(8,128)(2,1)S(1)}, u32[]{:S(2)}, u32[]{:S(2)}) %all-to-all-start.3) | async-done | bytes 1048608 | tf_op jit(solution)/shard_map/all_to_all | solution.py:63
  221.7 3.2 %all-to-all-start.4 = ((bf16[4,2,128]{2,1,0:T(2,128)(2,1)}), bf16[4,2,128]{2,1,0:T(2,128)(2,1)S(1)}, u32[]{:S(2)}, u32[]{:S(2)}) async-start(bf16[4,2,128]{2,1,0:T(2,128)(2,1)} %select_convert_fusion), calls=%async_computation.4 | async-start | bytes 4096 | tf_op jit(solution)/shard_map/all_to_all | solution.py:95
  224.9 1.5 copy.89
  226.4 1.4 multiply_reduce_fusion
  227.8 1.3 copy-done.4
  229.1 0.2 multiply_convert_fusion
  229.4 2.0 gather_fusion.2
  231.4 3.2 %select_select_fusion = bf16[4,2,128,1024]{3,2,1,0:T(8,128)(2,1)} fusion(bf16[4,2,128,1024]{3,2,1,0:T(8,128)(2,1)} %bitcast.118, pred[4,2]{1,0:T(4,128)(4,1)S(1)} %copy.94, pred[4,2]{1,0:T(4,128)(4,1)S(1)} %copy.90), kind=kLoop, calls=%fused_computation.25 | loop fusion | flops 2097152 | bytes 4194320 | tf_op jit(solution)/shard_map/jit(_where)/select_n | solution.py:84
  234.6 4.4 %all-to-all-start.5 = ((bf16[4,2,128,1024]{3,2,1,0:T(8,128)(2,1)}), bf16[4,2,128,1024]{3,2,1,0:T(8,128)(2,1)}, u32[]{:S(2)}, u32[]{:S(2)}) async-start(bf16[4,2,128,1024]{3,2,1,0:T(8,128)(2,1)} %select_select_fusion), calls=%async_computation.5 | async-start | bytes 4194304 | tf_op jit(solution)/shard_map/all_to_all | solution.py:94
  239.3 2.8 %fusion.56 = bf16[1,512,1024]{2,1,0:T(8,128)(2,1)} fusion(f32[1024]{0:T(1024)S(1)} %copy-done.10, f32[512,1024]{1,0:T(8,128)} %copy-done.4, f32[512]{0:T(512)S(1)} %add_rsqrt_fusion), kind=kLoop, calls=%fused_computation.59 | loop fusion | flops 1572864 | bytes 3151872 | tf_op jit(solution)/shard_map/broadcast_in_dim | solution.py:104
  242.1 22.7 %all-to-all-done.5 = bf16[4,2,128,1024]{3,2,1,0:T(8,128)(2,1)} async-done(((bf16[4,2,128,1024]{3,2,1,0:T(8,128)(2,1)}), bf16[4,2,128,1024]{3,2,1,0:T(8,128)(2,1)}, u32[]{:S(2)}, u32[]{:S(2)}) %all-to-all-start.5) | async-done | bytes 2097184 | tf_op jit(solution)/shard_map/all_to_all | solution.py:94
  264.8 2.8 %fusion.36 = bf16[1,128,1024]{2,1,0:T(8,128)(2,1)} fusion(bf16[4,2,128,1024]{3,2,1,0:T(8,128)(2,1)} %all-to-all-done.5, f32[128]{0:T(128)S(1)} %broadcast_maximum_fusion, bf16[4,2,128]{2,0,1:T(4,128)(2,1)S(1)} %copy.95, bf16[128]{0:T(256)(128)(2,1)S(1)} %iota_convert_fusion), kind=kOutput, calls=%fused_computation.35 | convolution fusion | flops 268828672 | bytes 2362112 | tf_op jit(solution)/shard_map/scrf,scfd->rd/dot_general | solution.py:99
  (57 shorter events, 3.1 us)
Async XLA Ops:
  0.6 225.8 %copy-start = (bf16[1024,1024]{1,0:T(8,128)(2,1)S(1)}, bf16[1024,1024]{1,0:T(8,128)(2,1)}, u32[]{:S(2)}) copy-start(bf16[1024,1024]{1,0:T(8,128)(2,1)} %param.13) | copy-start | bytes 6291460
  0.6 20.1 %copy-start.5 = (bf16[1,512,1024]{2,1,0:T(8,128)(2,1)S(1)}, bf16[1,512,1024]{2,1,0:T(8,128)(2,1)}, u32[]{:S(2)}) copy-start(bf16[1,512,1024]{2,1,0:T(8,128)(2,1)} %param.11) | copy-start | bytes 3145732
  13.5 37.5 %all-to-all-start.1 = ((bf16[256,8,128]{0,2,1:T(8,128)(2,1)}), bf16[256,8,128]{0,2,1:T(8,128)(2,1)}, u32[]{:S(2)}, u32[]{:S(2)}) async-start(bf16[256,8,128]{0,2,1:T(8,128)(2,1)} %bitcast.126), calls=%async_computation.1 | async-start | bytes 1048576 | tf_op jit(solution)/shard_map/all_to_all | solution.py:58
  22.1 12.7 %copy-start.7 = (bf16[1,512,1024]{1,2,0:T(8,128)(2,1)S(1)}, bf16[1,512,1024]{1,2,0:T(8,128)(2,1)}, u32[]{:S(2)}) copy-start(bf16[1,512,1024]{1,2,0:T(8,128)(2,1)} %copy.83) | copy-start | bytes 3145732
  37.2 3.2 %copy-start.3 = (f32[16,256,512]{2,1,0:T(8,128)}, f32[16,256,512]{2,1,0:T(8,128)S(1)}, u32[]{:S(2)}) copy-start(f32[16,256,512]{2,1,0:T(8,128)S(1)} %get-tuple-element.72) | copy-start | bytes 25165828
  42.5 14.5 %copy-start.6 = (bf16[1,512,1024]{2,1,0:T(8,128)(2,1)S(1)}, bf16[1,512,1024]{2,1,0:T(8,128)(2,1)}, u32[]{:S(2)}) copy-start(bf16[1,512,1024]{2,1,0:T(8,128)(2,1)} %param.10) | copy-start | bytes 3145732
  51.0 20.1 %all-to-all-start.2 = ((bf16[256,8,128]{0,2,1:T(8,128)(2,1)}), bf16[256,8,128]{0,2,1:T(8,128)(2,1)}, u32[]{:S(2)}, u32[]{:S(2)}) async-start(bf16[256,8,128]{0,2,1:T(8,128)(2,1)} %bitcast.131), calls=%async_computation.2 | async-start | bytes 1048576 | tf_op jit(solution)/shard_map/all_to_all | solution.py:59
  71.0 29.5 %all-to-all-start = ((bf16[512,8,128]{0,2,1:T(8,128)(2,1)}), bf16[512,8,128]{0,2,1:T(8,128)(2,1)}, u32[]{:S(2)}, u32[]{:S(2)}) async-start(bf16[512,8,128]{0,2,1:T(8,128)(2,1)} %bitcast.124), calls=%async_computation | async-start | bytes 2097152 | tf_op jit(solution)/shard_map/all_to_all | solution.py:57
  102.8 93.1 %copy-start.11 = (s32[1,4,1]{1,2,0:T(1,128)S(1)}, s32[1,4,1]{1,2,0:T(1,128)}, u32[]{:S(2)}) copy-start(s32[1,4,1]{1,2,0:T(1,128)} %param.15) | copy-start | bytes 52
  102.8 93.8 %copy-start.1 = (s32[1,4]{1,0:T(1,128)S(1)}, s32[1,4]{1,0:T(1,128)}, u32[]{:S(2)}) copy-start(s32[1,4]{1,0:T(1,128)} %param.16) | copy-start | bytes 52
  102.8 95.0 %copy-start.9 = (s32[1,4,128]{2,1,0:T(4,128)S(1)}, s32[1,4,128]{2,1,0:T(4,128)}, u32[]{:S(2)}) copy-start(s32[1,4,128]{2,1,0:T(4,128)} %param.17) | copy-start | bytes 6148
  106.5 5.7 %copy-start.2 = (f32[2,1024,2048]{2,1,0:T(8,128)}, f32[2,1024,2048]{2,1,0:T(8,128)S(1)}, u32[]{:S(2)}) copy-start(f32[2,1024,2048]{2,1,0:T(8,128)S(1)} %get-tuple-element.108) | copy-start | bytes 50331652 | tf_op jit(solution)/shard_map/while
  128.8 5.7 %copy-start.2 = (f32[2,1024,2048]{2,1,0:T(8,128)}, f32[2,1024,2048]{2,1,0:T(8,128)S(1)}, u32[]{:S(2)}) copy-start(f32[2,1024,2048]{2,1,0:T(8,128)S(1)} %get-tuple-element.108) | copy-start | bytes 50331652 | tf_op jit(solution)/shard_map/while
  151.1 5.7 %copy-start.2 = (f32[2,1024,2048]{2,1,0:T(8,128)}, f32[2,1024,2048]{2,1,0:T(8,128)S(1)}, u32[]{:S(2)}) copy-start(f32[2,1024,2048]{2,1,0:T(8,128)S(1)} %get-tuple-element.108) | copy-start | bytes 50331652 | tf_op jit(solution)/shard_map/while
  173.5 5.7 %copy-start.2 = (f32[2,1024,2048]{2,1,0:T(8,128)}, f32[2,1024,2048]{2,1,0:T(8,128)S(1)}, u32[]{:S(2)}) copy-start(f32[2,1024,2048]{2,1,0:T(8,128)S(1)} %get-tuple-element.108) | copy-start | bytes 50331652 | tf_op jit(solution)/shard_map/while
  192.2 36.9 %copy-start.10 = (f32[1024]{0:T(1024)S(1)}, f32[1024]{0:T(1024)}, u32[]{:S(2)}) copy-start(f32[1024]{0:T(1024)} %param.14) | copy-start | bytes 12292
  192.2 29.5 %all-to-all-start.3 = ((bf16[8,512,128]{2,1,0:T(8,128)(2,1)}), bf16[8,512,128]{2,1,0:T(8,128)(2,1)S(1)}, u32[]{:S(2)}, u32[]{:S(2)}) async-start(bf16[8,512,128]{2,1,0:T(8,128)(2,1)} %bitcast.128), calls=%async_computation.3 | async-start | bytes 2097152 | tf_op jit(solution)/shard_map/all_to_all | solution.py:63
  221.7 3.2 %copy-start.8 = (bf16[8,512,128]{2,1,0:T(8,128)(2,1)}, bf16[8,512,128]{2,1,0:T(8,128)(2,1)S(1)}, u32[]{:S(2)}) copy-start(bf16[8,512,128]{2,1,0:T(8,128)(2,1)S(1)} %all-to-all-done.3) | copy-start | bytes 3145732
  221.7 12.9 %all-to-all-start.4 = ((bf16[4,2,128]{2,1,0:T(2,128)(2,1)}), bf16[4,2,128]{2,1,0:T(2,128)(2,1)S(1)}, u32[]{:S(2)}, u32[]{:S(2)}) async-start(bf16[4,2,128]{2,1,0:T(2,128)(2,1)} %select_convert_fusion), calls=%async_computation.4 | async-start | bytes 4096 | tf_op jit(solution)/shard_map/all_to_all | solution.py:95
  227.8 1.4 copy-start.4
  234.6 30.2 %all-to-all-start.5 = ((bf16[4,2,128,1024]{3,2,1,0:T(8,128)(2,1)}), bf16[4,2,128,1024]{3,2,1,0:T(8,128)(2,1)}, u32[]{:S(2)}, u32[]{:S(2)}) async-start(bf16[4,2,128,1024]{3,2,1,0:T(8,128)(2,1)} %select_select_fusion), calls=%async_computation.5 | async-start | bytes 4194304 | tf_op jit(solution)/shard_map/all_to_all | solution.py:94
where the time goes:
time: 269 us; the launch traced here: 268 us
  waiting for transfers between devices  79.7 us (30%)
  local copies, waits for them, and re-layouts  62.9 us (23%)
  matrix products  58 us (22%)
  other arithmetic  37.1 us (14%)
  starting transfers between devices  28.9 us (11%)
    dot_general x5, matrix products, mix_heads(): jnp.einsum('nhm,mhe->nhe', weights.astype(jnp.bfloat16), value_heads, pre...  41.5 us
    while x8, local copies, waits for them, and re-layouts  22.9 us
    all_to_all x1, waiting for transfers between devices, local(): lax.all_to_all(sent_rows, 'pack', split_axis=0, concat_axis=0, tiled=True)  22.7 us
    all_to_all x1, waiting for transfers between devices, local(): lax.all_to_all(head_result, 'tm', split_axis=0, concat_axis=1, tiled=True)  22.5 us
    all_to_all x1, waiting for transfers between devices, local(): lax.all_to_all(frame_q, 'tm', split_axis=1, concat_axis=0, tiled=True)  21.8 us
    reduce_sum x5, other arithmetic, mix_heads(): totals = jnp.sum(weights, axis=-1)  15 us
    all_to_all x1, waiting for transfers between devices, local(): lax.all_to_all(mark_values, 'tm', split_axis=1, concat_axis=0, tiled=True)  12.7 us
    dot_general x5, matrix products, mix_heads(): jnp.einsum('nhe,mhe->nhm', query_heads, key_heads, preferred_element_type...  12.3 us
  transfers between devices with their start and end apart: 6, of which 4 were waited for; matrix products, arithmetic and copies ran while one was open for 17% of the time, Pallas kernels for 0%

commit v1 on v0

--- a/solution.py
+++ b/solution.py
@@ -8,6 +8,28 @@
 LANDMARKS = 256
 BLOCK = 128
 POOL_DEV = 128
+
+
+def split_up(shard, dim, size):
+    before, after = (shard.shape[:dim], shard.shape[dim + 1 :])
+    return jnp.moveaxis(shard.reshape(*before, size, -1, *after), dim, 0)
+
+
+def in_order(blocks, dim):
+    shape = list(blocks.shape[1:])
+    shape[dim] *= blocks.shape[0]
+    return jnp.moveaxis(blocks, 0, dim).reshape(shape)
+
+
+def pairwise_exchange(array, axis, split_dim, concat_dim):
+    count, index = (lax.axis_size(axis), lax.axis_index(axis))
+    tiles = split_up(array, split_dim, count)
+    outs = [tiles[index]]
+    for step in range(1, count):
+        sent = tiles[index ^ step]
+        outs.append(lax.ppermute(sent, axis, [(i, i ^ step) for i in range(count)]))
+    tiles = jnp.stack(outs)[index ^ jnp.arange(count)]
+    return in_order(tiles, concat_dim)
 
 
 def mix_heads(query_rows, mark_keys, mark_values, head_count):
@@ -56,7 +78,7 @@
     spread_q, spread_k, spread_v = (
         lax.all_to_all(frame_q, "tm", split_axis=1, concat_axis=0, tiled=True),
         lax.all_to_all(mark_keys, "tm", split_axis=1, concat_axis=0, tiled=True),
-        lax.all_to_all(mark_values, "tm", split_axis=1, concat_axis=0, tiled=True),
+        pairwise_exchange(mark_values, "tm", 1, 0),
     )
     local_heads = HEADS // lax.axis_size("tm")
     head_result = mix_blocked(spread_q, spread_k, spread_v, local_heads)

time: 269 us -> 257 us (0.955)
  waiting for transfers between devices: 79.7 us -> 60.4 us
  starting transfers between devices: 28.9 us -> 40.8 us
  local copies, waits for them, and re-layouts: 62.9 us -> 58.5 us
    all_to_all x1, waiting for transfers between devices: 21.8 us -> 1.64 us  [local(): lax.all_to_all(frame_q, 'tm', split_axis=1, concat_axis=0, tiled=True)]
    ppermute x0 -> x7, waiting for transfers between devices: none -> 13.7 us  [pairwise_exchange(): outs.append(lax.ppermute(sent, axis, [(i, i ^ step) for i in range(count)]))]
    ppermute x0 -> x7, starting transfers between devices: none -> 13.4 us  [pairwise_exchange(): outs.append(lax.ppermute(sent, axis, [(i, i ^ step) for i in range(count)]))]
    while x8, local copies, waits for them, and re-layouts: 22.9 us -> 9.79 us
    all_to_all x1 -> x0, waiting for transfers between devices: 12.7 us -> none  [local(): lax.all_to_all(mark_values, 'tm', split_axis=1, concat_axis=0, tiled=True)]
    another operation x0 -> x11, local copies, waits for them, and re-layouts: none -> 6.2 us
    all_to_all x1 -> x0, starting transfers between devices: 5.99 us -> none  [local(): lax.all_to_all(mark_values, 'tm', split_axis=1, concat_axis=0, tiled=True)]
    all_to_all x1, starting transfers between devices: 3.69 us -> 7.89 us  [local(): lax.all_to_all(head_result, 'tm', split_axis=0, concat_axis=1, tiled=True)]
  transfers between devices with their start and end apart: 6 -> 12, of which waited for: 4 -> 5; matrix products, arithmetic and copies ran while one was open for 17% -> 21% of each run, Pallas kernels for 0% -> 0%
where the time goes in v1:
time: 257 us; the launch traced here: 255 us
  waiting for transfers between devices  60.4 us (24%)
  local copies, waits for them, and re-layouts  58.5 us (23%)
  matrix products  57.2 us (22%)
  starting transfers between devices  40.8 us (16%)
  other arithmetic  37.1 us (14%)
    dot_general x5, matrix products, mix_heads(): jnp.einsum('nhm,mhe->nhe', weights.astype(jnp.bfloat16), value_heads, pre...  40.7 us
    all_to_all x1, waiting for transfers between devices, local(): lax.all_to_all(sent_rows, 'pack', split_axis=0, concat_axis=0, tiled=True)  22.7 us
    all_to_all x1, waiting for transfers between devices, local(): lax.all_to_all(head_result, 'tm', split_axis=0, concat_axis=1, tiled=True)  22.4 us
    reduce_sum x5, other arithmetic, mix_heads(): totals = jnp.sum(weights, axis=-1)  15.1 us
    ppermute x7, waiting for transfers between devices, pairwise_exchange(): outs.append(lax.ppermute(sent, axis, [(i, i ^ step) for i in range(count)]))  13.7 us
    ppermute x7, starting transfers between devices, pairwise_exchange(): outs.append(lax.ppermute(sent, axis, [(i, i ^ step) for i in range(count)]))  13.4 us
    unnamed x34, local copies, waits for them, and re-layouts  13.1 us
    dot_general x5, matrix products, mix_heads(): jnp.einsum('nhe,mhe->nhm', query_heads, key_heads, preferred_element_type...  12.3 us
  transfers between devices with their start and end apart: 12, of which 5 were waited for; matrix products, arithmetic and copies ran while one was open for 21% of the time, Pallas kernels for 0%

profile of v1, /device:TPU:0, one launch (start us, length us, event | category | flops | bytes accessed | tf_op | source)
XLA Modules:
  0.0 255.2 jit_solution(1806014621857053513)
XLA Ops:
  0.7 3.6 %reshape.191 = f32[256,2,1024]{2,1,0:T(2,128)} reshape(bf16[1,512,1024]{2,1,0:T(8,128)(2,1)} %param.11) | data formatting | bytes 3145728 | tf_op jit(solution)/shard_map/convert_element_type | solution.py:74
  4.2 5.1 %reduce_sum.74 = f32[256,1024]{1,0:T(8,128)} reduce(f32[256,2,1024]{2,1,0:T(2,128)} %reshape.191, f32[]{:T(128)} %constant.45.clone.1), dimensions={1}, to_apply=%region_0.0 | reduce | flops 262144 | bytes 3145732 | tf_op jit(solution)/shard_map/reduce_sum | solution.py:74
  9.3 2.1 multiply_convert_fusion.2
  11.4 2.1 copy.111
  13.4 7.3 %all-to-all-start.1 = ((bf16[256,8,128]{0,2,1:T(8,128)(2,1)}), bf16[256,8,128]{0,2,1:T(8,128)(2,1)}, u32[]{:S(2)}, u32[]{:S(2)}) async-start(bf16[256,8,128]{0,2,1:T(8,128)(2,1)} %bitcast.157), calls=%async_computation.1 | async-start | bytes 1048576 | tf_op jit(solution)/shard_map/all_to_all | solution.py:80
  20.7 1.3 copy.114
  22.1 3.5 %reshape.192 = f32[256,2,1024]{2,1,0:T(2,128)} reshape(bf16[1,512,1024]{2,1,0:T(8,128)(2,1)} %param.10) | data formatting | bytes 3145728 | tf_op jit(solution)/shard_map/convert_element_type | solution.py:71
  25.5 5.1 %reduce_sum.75 = f32[256,1024]{1,0:T(8,128)} reduce(f32[256,2,1024]{2,1,0:T(2,128)} %reshape.192, f32[]{:T(128)} %constant.45.clone.1), dimensions={1}, to_apply=%region_1.0 | reduce | flops 262144 | bytes 3145732 | tf_op jit(solution)/shard_map/reduce_sum | solution.py:71
  30.6 2.1 multiply_convert_fusion.1
  32.7 2.0 copy.113
  34.7 2.4 bitcast_reduce_fusion.1
  37.2 3.2 %copy-done.3 = f32[16,256,512]{2,1,0:T(8,128)} copy-done((f32[16,256,512]{2,1,0:T(8,128)}, f32[16,256,512]{2,1,0:T(8,128)S(1)}, u32[]{:S(2)}) %copy-start.3) | copy-done | bytes 8388632
  40.4 2.0 fusion.16
  42.4 2.4 copy.115
  44.8 5.3 %divide_convert_fusion = bf16[256,16,64]{0,2,1:T(8,128)(2,1)S(1)} fusion(bf16[512,16,64]{0,2,1:T(8,128)(2,1)} %bitcast.160, f32[16,256,512]{2,1,0:T(8,128)} %copy-done.3, f32[256,16]{0,1:T(8,128)S(1)} %get-tuple-element.79, f32[256,16]{0,1:T(8,128)S(1)} %fusion.16), kind=kOutput, calls=%fused_computation.31 | convolution fusion | flops 275251200 | bytes 9994240 | tf_op jit(solution)/shard_map/nhm,mhe->nhe/dot_general | solution.py:46
  50.8 1.6 copy.117
  52.4 2.0 collective-permute-start
  54.4 1.6 copy.118
  56.0 1.5 collective-permute-start.1
  58.3 3.0 %collective-permute-start.3 = (bf16[256,128]{1,0:T(8,128)(2,1)S(1)}, bf16[256,128]{1,0:T(8,128)(2,1)}, u32[]{:S(2)}, u32[]{:S(2)}) collective-permute-start(bf16[256,128]{1,0:T(8,128)(2,1)S(1)} %bitcast.164), channel_id=1, source_target_pairs={{0,16},{4,20},{8,24},{12,28},{16,0},{20,4},{24,8},{28,12},{1,17},{... | collective-permute-start | bytes 196616 | tf_op jit(solution)/shard_map/ppermute | solution.py:30
  61.4 1.5 collective-permute-start.4
  62.9 1.3 copy.109
  64.4 4.6 %all-to-all-start = ((bf16[512,8,128]{0,2,1:T(8,128)(2,1)}), bf16[512,8,128]{0,2,1:T(8,128)(2,1)}, u32[]{:S(2)}, u32[]{:S(2)}) async-start(bf16[512,8,128]{0,2,1:T(8,128)(2,1)} %bitcast.154), calls=%async_computation | async-start | bytes 2097152 | tf_op jit(solution)/shard_map/all_to_all | solution.py:79
  69.2 3.9 %collective-permute-start.5 = (bf16[256,128]{1,0:T(8,128)(2,1)S(1)}, bf16[256,128]{1,0:T(8,128)(2,1)S(1)}, u32[]{:S(2)}, u32[]{:S(2)}) collective-permute-start(bf16[256,128]{1,0:T(8,128)(2,1)S(1)} %bitcast.169), channel_id=1, source_target_pairs={{0,24},{4,28},{8,16},{12,20},{16,8},{20,12},{24,0},{28,4},{1,25},{... | collective-permute-start | bytes 196616 | tf_op jit(solution)/shard_map/ppermute | solution.py:30
  74.0 1.5 collective-permute-start.6
  78.1 12.1 %collective-permute-done.5 = bf16[256,128]{1,0:T(8,128)(2,1)S(1)} collective-permute-done((bf16[256,128]{1,0:T(8,128)(2,1)S(1)}, bf16[256,128]{1,0:T(8,128)(2,1)S(1)}, u32[]{:S(2)}, u32[]{:S(2)}) %collective-permute-start.5) | collective-permute-done | bytes 65568 | tf_op jit(solution)/shard_map/ppermute | solution.py:30
  90.3 1.6 collective-permute-done.6
  92.9 1.1 reshape_reshape.3
  94.0 1.3 copy.112
  95.5 1.6 all-to-all-done
  97.2 2.3 copy.110
  99.4 76.4 %while.11 = (s32[]{:T(128)}, bf16[4,1024,128]{2,1,0:T(8,128)(2,1)}, bf16[4,1024,128]{2,1,0:T(8,128)(2,1)}, bf16[2048,128]{0,1:T(8,128)(2,1)S(1)}, bf16[8,256,128...) while((s32[]{:T(128)}, bf16[4,1024,128]{2,1,0:T(8,128)(2,1)}, ...), condition=%wide.wide.region_7.8_spmd, body=%wide.wide.region_4.7_spmd.sunk | while | flops 1107554304 | bytes 121152104 | solution.py:59
  99.5 1.0 constant_dynamic-slice_fusion.11
  100.6 2.5 bitcast_reduce_fusion.4
  103.1 3.3 %fusion.74 = f32[1024,2]{0,1:T(2,128)S(1)} fusion(f32[2,1024,2048]{2,1,0:T(8,128)S(1)} %get-tuple-element.144, f32[1024,2]{0,1:T(2,128)S(1)} %get-tuple-element.145), kind=kLoop, calls=%fused_computation.7.clone.clone.1 | loop fusion | flops 12580864 | bytes 16793600 | tf_op jit(solution)/shard_map/while/body/eval_jaxpr/reduce_sum | solution.py:45
  106.4 2.4 copy-done.2
  108.8 8.8 %fusion.75 = bf16[1024,2,64]{0,2,1:T(8,128)(2,1)S(1)} fusion(bf16[2048,2,64]{0,2,1:T(8,128)(2,1)} %get-tuple-element.165, f32[2,1024,2048]{2,1,0:T(8,128)} %copy-done.2, f32[1024,2]{0,1:T(2,128)S(1)} %get-tuple-element.145, f32[1024,2]{0,1:T(2,128)S(1)} %fusion.74), kind=kOutput, calls=%fused_computation.12.clone.clone.1 | convolution fusion | flops 549715968 | bytes 17580032 | tf_op jit(solution)/shard_map/while/body/eval_jaxpr/nhm,mhe->nhe/dot_general | solution.py:46
  118.6 1.0 constant_dynamic-slice_fusion.11
  119.7 2.5 bitcast_reduce_fusion.4
  122.2 3.3 %fusion.74 = f32[1024,2]{0,1:T(2,128)S(1)} fusion(f32[2,1024,2048]{2,1,0:T(8,128)S(1)} %get-tuple-element.144, f32[1024,2]{0,1:T(2,128)S(1)} %get-tuple-element.145), kind=kLoop, calls=%fused_computation.7.clone.clone.1 | loop fusion | flops 12580864 | bytes 16793600 | tf_op jit(solution)/shard_map/while/body/eval_jaxpr/reduce_sum | solution.py:45
  125.5 2.4 copy-done.2
  127.9 8.8 %fusion.75 = bf16[1024,2,64]{0,2,1:T(8,128)(2,1)S(1)} fusion(bf16[2048,2,64]{0,2,1:T(8,128)(2,1)} %get-tuple-element.165, f32[2,1024,2048]{2,1,0:T(8,128)} %copy-done.2, f32[1024,2]{0,1:T(2,128)S(1)} %get-tuple-element.145, f32[1024,2]{0,1:T(2,128)S(1)} %fusion.74), kind=kOutput, calls=%fused_computation.12.clone.clone.1 | convolution fusion | flops 549715968 | bytes 17580032 | tf_op jit(solution)/shard_map/while/body/eval_jaxpr/nhm,mhe->nhe/dot_general | solution.py:46
  137.7 1.0 constant_dynamic-slice_fusion.11
  138.8 2.5 bitcast_reduce_fusion.4
  141.3 3.3 %fusion.74 = f32[1024,2]{0,1:T(2,128)S(1)} fusion(f32[2,1024,2048]{2,1,0:T(8,128)S(1)} %get-tuple-element.144, f32[1024,2]{0,1:T(2,128)S(1)} %get-tuple-element.145), kind=kLoop, calls=%fused_computation.7.clone.clone.1 | loop fusion | flops 12580864 | bytes 16793600 | tf_op jit(solution)/shard_map/while/body/eval_jaxpr/reduce_sum | solution.py:45
  144.5 2.4 copy-done.2
  147.0 8.8 %fusion.75 = bf16[1024,2,64]{0,2,1:T(8,128)(2,1)S(1)} fusion(bf16[2048,2,64]{0,2,1:T(8,128)(2,1)} %get-tuple-element.165, f32[2,1024,2048]{2,1,0:T(8,128)} %copy-done.2, f32[1024,2]{0,1:T(2,128)S(1)} %get-tuple-element.145, f32[1024,2]{0,1:T(2,128)S(1)} %fusion.74), kind=kOutput, calls=%fused_computation.12.clone.clone.1 | convolution fusion | flops 549715968 | bytes 17580032 | tf_op jit(solution)/shard_map/while/body/eval_jaxpr/nhm,mhe->nhe/dot_general | solution.py:46
  156.7 1.0 constant_dynamic-slice_fusion.11
  157.9 2.5 bitcast_reduce_fusion.4
  160.4 3.3 %fusion.74 = f32[1024,2]{0,1:T(2,128)S(1)} fusion(f32[2,1024,2048]{2,1,0:T(8,128)S(1)} %get-tuple-element.144, f32[1024,2]{0,1:T(2,128)S(1)} %get-tuple-element.145), kind=kLoop, calls=%fused_computation.7.clone.clone.1 | loop fusion | flops 12580864 | bytes 16793600 | tf_op jit(solution)/shard_map/while/body/eval_jaxpr/reduce_sum | solution.py:45
  163.6 2.4 copy-done.2
  166.1 8.8 %fusion.75 = bf16[1024,2,64]{0,2,1:T(8,128)(2,1)S(1)} fusion(bf16[2048,2,64]{0,2,1:T(8,128)(2,1)} %get-tuple-element.165, f32[2,1024,2048]{2,1,0:T(8,128)} %copy-done.2, f32[1024,2]{0,1:T(2,128)S(1)} %get-tuple-element.145, f32[1024,2]{0,1:T(2,128)S(1)} %fusion.74), kind=kOutput, calls=%fused_computation.12.clone.clone.1 | convolution fusion | flops 549715968 | bytes 17580032 | tf_op jit(solution)/shard_map/while/body/eval_jaxpr/nhm,mhe->nhe/dot_general | solution.py:46
  175.8 7.9 %all-to-all-start.2 = ((bf16[8,512,128]{2,1,0:T(8,128)(2,1)}), bf16[8,512,128]{2,1,0:T(8,128)(2,1)S(1)}, u32[]{:S(2)}, u32[]{:S(2)}) async-start(bf16[8,512,128]{2,1,0:T(8,128)(2,1)} %bitcast.159), calls=%async_computation.2 | async-start | bytes 2097152 | tf_op jit(solution)/shard_map/all_to_all | solution.py:85
  186.9 22.4 %all-to-all-done.2 = bf16[8,512,128]{2,1,0:T(8,128)(2,1)S(1)} async-done(((bf16[8,512,128]{2,1,0:T(8,128)(2,1)}), bf16[8,512,128]{2,1,0:T(8,128)(2,1)S(1)}, u32[]{:S(2)}, u32[]{:S(2)}) %all-to-all-start.2) | async-done | bytes 1048608 | tf_op jit(solution)/shard_map/all_to_all | solution.py:85
  209.3 3.2 %all-to-all-start.3 = ((bf16[4,2,128]{2,1,0:T(2,128)(2,1)}), bf16[4,2,128]{2,1,0:T(2,128)(2,1)S(1)}, u32[]{:S(2)}, u32[]{:S(2)}) async-start(bf16[4,2,128]{2,1,0:T(2,128)(2,1)} %select_convert_fusion), calls=%async_computation.3 | async-start | bytes 4096 | tf_op jit(solution)/shard_map/all_to_all | solution.py:117
  212.5 1.5 copy.128
  214.0 1.4 multiply_reduce_fusion
  215.4 1.3 copy-done.4
  217.0 2.0 gather_fusion.3
  219.0 3.2 %select_select_fusion = bf16[4,2,128,1024]{3,2,1,0:T(8,128)(2,1)} fusion(bf16[4,2,128,1024]{3,2,1,0:T(8,128)(2,1)} %bitcast.149, pred[4,2]{1,0:T(4,128)(4,1)S(1)} %copy.133, pred[4,2]{1,0:T(4,128)(4,1)S(1)} %copy.129), kind=kLoop, calls=%fused_computation.26 | loop fusion | flops 2097152 | bytes 4194320 | tf_op jit(solution)/shard_map/jit(_where)/select_n | solution.py:106
  222.2 4.4 %all-to-all-start.4 = ((bf16[4,2,128,1024]{3,2,1,0:T(8,128)(2,1)}), bf16[4,2,128,1024]{3,2,1,0:T(8,128)(2,1)}, u32[]{:S(2)}, u32[]{:S(2)}) async-start(bf16[4,2,128,1024]{3,2,1,0:T(8,128)(2,1)} %select_select_fusion), calls=%async_computation.4 | async-start | bytes 4194304 | tf_op jit(solution)/shard_map/all_to_all | solution.py:116
  226.9 2.8 %fusion.57 = bf16[1,512,1024]{2,1,0:T(8,128)(2,1)} fusion(f32[1024]{0:T(1024)S(1)} %copy-done.11, f32[512,1024]{1,0:T(8,128)} %copy-done.4, f32[512]{0:T(512)S(1)} %add_rsqrt_fusion), kind=kLoop, calls=%fused_computation.79 | loop fusion | flops 1572864 | bytes 3151872 | tf_op jit(solution)/shard_map/broadcast_in_dim | solution.py:126
  229.7 22.7 %all-to-all-done.4 = bf16[4,2,128,1024]{3,2,1,0:T(8,128)(2,1)} async-done(((bf16[4,2,128,1024]{3,2,1,0:T(8,128)(2,1)}), bf16[4,2,128,1024]{3,2,1,0:T(8,128)(2,1)}, u32[]{:S(2)}, u32[]{:S(2)}) %all-to-all-start.4) | async-done | bytes 2097184 | tf_op jit(solution)/shard_map/all_to_all | solution.py:116
  252.4 2.8 %fusion.36 = bf16[1,128,1024]{2,1,0:T(8,128)(2,1)} fusion(bf16[4,2,128,1024]{3,2,1,0:T(8,128)(2,1)} %all-to-all-done.4, f32[128]{0:T(128)S(1)} %broadcast_maximum_fusion, bf16[4,2,128]{2,0,1:T(4,128)(2,1)S(1)} %copy.134, bf16[128]{0:T(256)(128)(2,1)S(1)} %iota_convert_fusion), kind=kOutput, calls=%fused_computation.36 | convolution fusion | flops 268828672 | bytes 2362112 | tf_op jit(solution)/shard_map/scrf,scfd->rd/dot_general | solution.py:121
  (92 shorter events, 14.7 us)
Async XLA Ops:
  0.6 213.4 %copy-start = (bf16[1024,1024]{1,0:T(8,128)(2,1)S(1)}, bf16[1024,1024]{1,0:T(8,128)(2,1)}, u32[]{:S(2)}) copy-start(bf16[1024,1024]{1,0:T(8,128)(2,1)} %param.13) | copy-start | bytes 6291460
  0.6 20.1 %copy-start.5 = (bf16[1,512,1024]{2,1,0:T(8,128)(2,1)S(1)}, bf16[1,512,1024]{2,1,0:T(8,128)(2,1)}, u32[]{:S(2)}) copy-start(bf16[1,512,1024]{2,1,0:T(8,128)(2,1)} %param.11) | copy-start | bytes 3145732
  13.4 50.9 %all-to-all-start.1 = ((bf16[256,8,128]{0,2,1:T(8,128)(2,1)}), bf16[256,8,128]{0,2,1:T(8,128)(2,1)}, u32[]{:S(2)}, u32[]{:S(2)}) async-start(bf16[256,8,128]{0,2,1:T(8,128)(2,1)} %bitcast.157), calls=%async_computation.1 | async-start | bytes 1048576 | tf_op jit(solution)/shard_map/all_to_all | solution.py:80
  22.1 12.7 %copy-start.7 = (bf16[1,512,1024]{1,2,0:T(8,128)(2,1)S(1)}, bf16[1,512,1024]{1,2,0:T(8,128)(2,1)}, u32[]{:S(2)}) copy-start(bf16[1,512,1024]{1,2,0:T(8,128)(2,1)} %copy.114) | copy-start | bytes 3145732
  37.2 3.2 %copy-start.3 = (f32[16,256,512]{2,1,0:T(8,128)}, f32[16,256,512]{2,1,0:T(8,128)S(1)}, u32[]{:S(2)}) copy-start(f32[16,256,512]{2,1,0:T(8,128)S(1)} %get-tuple-element.80) | copy-start | bytes 25165828
  42.4 20.5 %copy-start.6 = (bf16[1,512,1024]{2,1,0:T(8,128)(2,1)S(1)}, bf16[1,512,1024]{2,1,0:T(8,128)(2,1)}, u32[]{:S(2)}) copy-start(bf16[1,512,1024]{2,1,0:T(8,128)(2,1)} %param.10) | copy-start | bytes 3145732
  52.4 16.8 %collective-permute-start = (bf16[256,128]{1,0:T(8,128)(2,1)}, bf16[256,128]{1,0:T(8,128)(2,1)}, u32[]{:S(2)}, u32[]{:S(2)}) collective-permute-start(bf16[256,128]{1,0:T(8,128)(2,1)} %bitcast.167), channel_id=1, source_target_pairs={{0,4},{4,0},{8,12},{12,8},{16,20},{20,16},{24,28},{28,24},{1,5},{5... | collective-permute-start | bytes 196616 | tf_op jit(solution)/shard_map/ppermute | solution.py:30
  56.0 18.0 %collective-permute-start.1 = (bf16[256,128]{1,0:T(8,128)(2,1)}, bf16[256,128]{1,0:T(8,128)(2,1)}, u32[]{:S(2)}, u32[]{:S(2)}) collective-permute-start(bf16[256,128]{1,0:T(8,128)(2,1)} %bitcast.166), channel_id=1, source_target_pairs={{0,8},{4,12},{8,0},{12,4},{16,24},{20,28},{24,16},{28,20},{1,9},{5... | collective-permute-start | bytes 196616 | tf_op jit(solution)/shard_map/ppermute | solution.py:30
  58.2 18.2 %collective-permute-start.2 = (bf16[256,128]{1,0:T(8,128)(2,1)}, bf16[256,128]{1,0:T(8,128)(2,1)}, u32[]{:S(2)}, u32[]{:S(2)}) collective-permute-start(bf16[256,128]{1,0:T(8,128)(2,1)} %bitcast.165), channel_id=1, source_target_pairs={{0,12},{4,8},{8,4},{12,0},{16,28},{20,24},{24,20},{28,16},{1,13},{... | collective-permute-start | bytes 196616 | tf_op jit(solution)/shard_map/ppermute | solution.py:30
  58.3 18.9 %collective-permute-start.3 = (bf16[256,128]{1,0:T(8,128)(2,1)S(1)}, bf16[256,128]{1,0:T(8,128)(2,1)}, u32[]{:S(2)}, u32[]{:S(2)}) collective-permute-start(bf16[256,128]{1,0:T(8,128)(2,1)S(1)} %bitcast.164), channel_id=1, source_target_pairs={{0,16},{4,20},{8,24},{12,28},{16,0},{20,4},{24,8},{28,12},{1,17},{... | collective-permute-start | bytes 196616 | tf_op jit(solution)/shard_map/ppermute | solution.py:30
  61.4 16.7 %collective-permute-start.4 = (bf16[256,128]{1,0:T(8,128)(2,1)S(1)}, bf16[256,128]{1,0:T(8,128)(2,1)S(1)}, u32[]{:S(2)}, u32[]{:S(2)}) collective-permute-start(bf16[256,128]{1,0:T(8,128)(2,1)S(1)} %bitcast.163), channel_id=1, source_target_pairs={{0,20},{4,16},{8,28},{12,24},{16,4},{20,0},{24,12},{28,8},{1,21},{... | collective-permute-start | bytes 196616 | tf_op jit(solution)/shard_map/ppermute | solution.py:30
  64.4 32.8 %all-to-all-start = ((bf16[512,8,128]{0,2,1:T(8,128)(2,1)}), bf16[512,8,128]{0,2,1:T(8,128)(2,1)}, u32[]{:S(2)}, u32[]{:S(2)}) async-start(bf16[512,8,128]{0,2,1:T(8,128)(2,1)} %bitcast.154), calls=%async_computation | async-start | bytes 2097152 | tf_op jit(solution)/shard_map/all_to_all | solution.py:79
  69.2 21.0 %collective-permute-start.5 = (bf16[256,128]{1,0:T(8,128)(2,1)S(1)}, bf16[256,128]{1,0:T(8,128)(2,1)S(1)}, u32[]{:S(2)}, u32[]{:S(2)}) collective-permute-start(bf16[256,128]{1,0:T(8,128)(2,1)S(1)} %bitcast.169), channel_id=1, source_target_pairs={{0,24},{4,28},{8,16},{12,20},{16,8},{20,12},{24,0},{28,4},{1,25},{... | collective-permute-start | bytes 196616 | tf_op jit(solution)/shard_map/ppermute | solution.py:30
  74.0 17.8 %collective-permute-start.6 = (bf16[256,128]{1,0:T(8,128)(2,1)S(1)}, bf16[256,128]{1,0:T(8,128)(2,1)S(1)}, u32[]{:S(2)}, u32[]{:S(2)}) collective-permute-start(bf16[256,128]{1,0:T(8,128)(2,1)S(1)} %bitcast.168), channel_id=1, source_target_pairs={{0,28},{4,24},{8,20},{12,16},{16,12},{20,8},{24,4},{28,0},{1,29},{... | collective-permute-start | bytes 196616 | tf_op jit(solution)/shard_map/ppermute | solution.py:30
  92.9 2.4 copy-start.9
  99.4 84.3 %copy-start.12 = (s32[1,4,1]{1,2,0:T(1,128)S(1)}, s32[1,4,1]{1,2,0:T(1,128)}, u32[]{:S(2)}) copy-start(s32[1,4,1]{1,2,0:T(1,128)} %param.15) | copy-start | bytes 52
  99.4 85.0 %copy-start.1 = (s32[1,4]{1,0:T(1,128)S(1)}, s32[1,4]{1,0:T(1,128)}, u32[]{:S(2)}) copy-start(s32[1,4]{1,0:T(1,128)} %param.16) | copy-start | bytes 52
  99.4 86.3 %copy-start.10 = (s32[1,4,128]{2,1,0:T(4,128)S(1)}, s32[1,4,128]{2,1,0:T(4,128)}, u32[]{:S(2)}) copy-start(s32[1,4,128]{2,1,0:T(4,128)} %param.17) | copy-start | bytes 6148
  103.1 5.7 %copy-start.2 = (f32[2,1024,2048]{2,1,0:T(8,128)}, f32[2,1024,2048]{2,1,0:T(8,128)S(1)}, u32[]{:S(2)}) copy-start(f32[2,1024,2048]{2,1,0:T(8,128)S(1)} %get-tuple-element.144) | copy-start | bytes 50331652 | tf_op jit(solution)/shard_map/while
  122.2 5.7 %copy-start.2 = (f32[2,1024,2048]{2,1,0:T(8,128)}, f32[2,1024,2048]{2,1,0:T(8,128)S(1)}, u32[]{:S(2)}) copy-start(f32[2,1024,2048]{2,1,0:T(8,128)S(1)} %get-tuple-element.144) | copy-start | bytes 50331652 | tf_op jit(solution)/shard_map/while
  141.3 5.7 %copy-start.2 = (f32[2,1024,2048]{2,1,0:T(8,128)}, f32[2,1024,2048]{2,1,0:T(8,128)S(1)}, u32[]{:S(2)}) copy-start(f32[2,1024,2048]{2,1,0:T(8,128)S(1)} %get-tuple-element.144) | copy-start | bytes 50331652 | tf_op jit(solution)/shard_map/while
  160.3 5.7 %copy-start.2 = (f32[2,1024,2048]{2,1,0:T(8,128)}, f32[2,1024,2048]{2,1,0:T(8,128)S(1)}, u32[]{:S(2)}) copy-start(f32[2,1024,2048]{2,1,0:T(8,128)S(1)} %get-tuple-element.144) | copy-start | bytes 50331652 | tf_op jit(solution)/shard_map/while
  175.8 40.9 %copy-start.11 = (f32[1024]{0:T(1024)S(1)}, f32[1024]{0:T(1024)}, u32[]{:S(2)}) copy-start(f32[1024]{0:T(1024)} %param.14) | copy-start | bytes 12292
  175.8 33.5 %all-to-all-start.2 = ((bf16[8,512,128]{2,1,0:T(8,128)(2,1)}), bf16[8,512,128]{2,1,0:T(8,128)(2,1)S(1)}, u32[]{:S(2)}, u32[]{:S(2)}) async-start(bf16[8,512,128]{2,1,0:T(8,128)(2,1)} %bitcast.159), calls=%async_computation.2 | async-start | bytes 2097152 | tf_op jit(solution)/shard_map/all_to_all | solution.py:85
  209.3 3.2 %copy-start.8 = (bf16[8,512,128]{2,1,0:T(8,128)(2,1)}, bf16[8,512,128]{2,1,0:T(8,128)(2,1)S(1)}, u32[]{:S(2)}) copy-start(bf16[8,512,128]{2,1,0:T(8,128)(2,1)S(1)} %all-to-all-done.2) | copy-start | bytes 3145732
  209.3 12.9 %all-to-all-start.3 = ((bf16[4,2,128]{2,1,0:T(2,128)(2,1)}), bf16[4,2,128]{2,1,0:T(2,128)(2,1)S(1)}, u32[]{:S(2)}, u32[]{:S(2)}) async-start(bf16[4,2,128]{2,1,0:T(2,128)(2,1)} %select_convert_fusion), calls=%async_computation.3 | async-start | bytes 4096 | tf_op jit(solution)/shard_map/all_to_all | solution.py:117
  215.4 1.3 copy-start.4
  222.2 30.2 %all-to-all-start.4 = ((bf16[4,2,128,1024]{3,2,1,0:T(8,128)(2,1)}), bf16[4,2,128,1024]{3,2,1,0:T(8,128)(2,1)}, u32[]{:S(2)}, u32[]{:S(2)}) async-start(bf16[4,2,128,1024]{3,2,1,0:T(8,128)(2,1)} %select_select_fusion), calls=%async_computation.4 | async-start | bytes 4194304 | tf_op jit(solution)/shard_map/all_to_all | solution.py:116
